TPU v7x, 32 devices: a whole 2x2x4 slice. The times are simulated.
32 devices in a mesh: fsdp: 8 (over z, x), replica: 4 (over y, core).
Axes of the slice: x: 2, y: 2, z: 4, core: 2. Of those that a mesh axis runs over, the one named last changes fastest.
Arguments:
- layer_input: bfloat16 [32, 1024, 768], P(('fsdp', 'replica')), may hold values from -6 to 6
- cotangent: bfloat16 [32, 1024, 768], P(('fsdp', 'replica')), may hold values from -6 to 6
- segment_ids: int32 [32, 1024], P(('fsdp', 'replica')), may hold values from 0 to 4, as said below
- pad_mask: int32 [32, 1024], P(('fsdp', 'replica')), may hold values from 0 to 1, as said below
- ln1_gain: bfloat16 [768], P('fsdp'), may hold values from 0.5 to 1.5
- ln1_bias: bfloat16 [768], P('fsdp'), may hold values from -1.1953125 to 1.1953125
- w_qkv: bfloat16 [768, 2304], P('fsdp'), may hold values from -0.21875 to 0.21875
- b_qkv: bfloat16 [2304], P('fsdp'), may hold values from -1.1953125 to 1.1953125
- w_out: bfloat16 [768, 768], P('fsdp'), may hold values from -1.25 to 1.25
- b_out: bfloat16 [768], P('fsdp'), may hold values from -1.1953125 to 1.1953125
- ln2_gain: bfloat16 [768], P('fsdp'), may hold values from 0.5 to 1.5
- ln2_bias: bfloat16 [768], P('fsdp'), may hold values from -1.1953125 to 1.1953125
- w_up: bfloat16 [768, 3072], P('fsdp'), may hold values from -0.21875 to 0.21875
- b_up: bfloat16 [3072], P('fsdp'), may hold values from -1.1953125 to 1.1953125
- w_down: bfloat16 [3072, 768], P('fsdp'), may hold values from -0.109375 to 0.109375
- b_down: bfloat16 [768], P('fsdp'), may hold values from -1.1953125 to 1.1953125
Outputs:
- layer_out: bfloat16 [32, 1024, 768], P(('fsdp', 'replica'))
- input_grad: bfloat16 [32, 1024, 768], P(('fsdp', 'replica'))
- grad_ln1_gain: float32 [768], P('fsdp')
- grad_ln1_bias: float32 [768], P('fsdp')
- grad_w_qkv: float32 [768, 2304], P('fsdp')
- grad_b_qkv: float32 [2304], P('fsdp')
- grad_w_out: float32 [768, 768], P('fsdp')
- grad_b_out: float32 [768], P('fsdp')
- grad_ln2_gain: float32 [768], P('fsdp')
- grad_ln2_bias: float32 [768], P('fsdp')
- grad_w_up: float32 [768, 3072], P('fsdp')
- grad_b_up: float32 [3072], P('fsdp')
- grad_w_down: float32 [3072, 768], P('fsdp')
- grad_b_down: float32 [768], P('fsdp')
Inputs may be any that keep to these rules, and one draw needn't show every extreme that they name: `segment_ids`: each row packs 4 genes numbered 0 to 3 in order from its start, each of 128 to 256 codons, never falling along a row, and 4 on the padded tail; in every row one gene has exactly 256 codons and another exactly 128. `pad_mask`: 1 exactly where segment_ids is under 4; every row ends in at least 128 padded codons.
All inputs are finite; a program needn't handle non-finite values.
Results may differ from a plain program's by a relative error of at most 0.014.
Values may be sent and summed in bfloat16 or wider, within the bound.
No kernel may reach another device: no remote copies, remote signals or barrier semaphores. Data moves between devices by JAX's collectives and lax.ppermute only.
A program may use at most 320 MiB of HBM per device.

v0:
```python
import math
import jax
import jax.numpy as jnp
from jax import lax
from jax.sharding import PartitionSpec as P

HEADS = 12
HEAD_DIM = 64
GENES = 4
EPSILON = 1e-05
NEG_FILL = -1000000000.0


def contract_rows(left_matrix, right_matrix):
    return lax.dot_general(
        left_matrix, right_matrix, (((0,), (0,)), ((), ())), preferred_element_type=jnp.float32
    )


def times_transpose(left_matrix, right_matrix):
    return lax.dot_general(
        left_matrix, right_matrix, (((1,), (1,)), ((), ())), preferred_element_type=jnp.float32
    )


def layer_norm(inputs, gain_vector, bias_vector):
    centered = inputs - jnp.mean(inputs, -1, keepdims=True)
    variance = jnp.mean(centered * centered, -1, keepdims=True)
    return centered * lax.rsqrt(variance + EPSILON) * gain_vector + bias_vector


def rotate(tensor, cosine_table, sine_table):
    half_dim = tensor.shape[-1] // 2
    first_half = tensor[..., :half_dim]
    second_half = tensor[..., half_dim:]
    return jnp.concatenate(
        [
            first_half * cosine_table - second_half * sine_table,
            second_half * cosine_table + first_half * sine_table,
        ],
        -1,
    )


def exact_gelu(inputs):
    return jax.nn.gelu(inputs, approximate=False)


def rotary_tables(positions):
    frequency = jnp.power(10000.0, jnp.arange(HEAD_DIM // 2, dtype=jnp.float32) * (-2.0 / HEAD_DIM))
    angles = positions.astype(jnp.float32)[..., None] * frequency
    return (jnp.cos(angles)[..., None, :], jnp.sin(angles)[..., None, :])


def gene_positions(segments):
    slot_ids = jnp.arange(GENES + 1, dtype=jnp.int32)
    slot_hits = segments[..., :, None] == slot_ids
    counts = jnp.sum(slot_hits.astype(jnp.int32), -2)
    starts = jnp.cumsum(counts, -1) - counts
    gene_start = jnp.sum(jnp.where(slot_hits, starts[..., None, :], 0), -1)
    return jnp.arange(segments.shape[-1], dtype=jnp.int32) - gene_start


def pair_mask(block_segments, block_valid, block_start, segments, valid_codons):
    row_ids = block_start + jnp.arange(block_segments.shape[0], dtype=jnp.int32)
    column_ids = jnp.arange(segments.shape[0], dtype=jnp.int32)
    same_gene = (
        (block_segments[:, None] == segments[None, :])
        & (block_valid[:, None] > 0)
        & (valid_codons[None, :] > 0)
    )
    return same_gene | (row_ids[:, None] == column_ids[None, :])


def block_scores(
    block_queries, key_rows, block_segments, block_valid, block_start, segments, valid_codons
):
    scores = jnp.einsum(
        "qhd,khd->hqk", block_queries, key_rows, preferred_element_type=jnp.float32
    ) * (1.0 / math.sqrt(HEAD_DIM))
    allowed = pair_mask(block_segments, block_valid, block_start, segments, valid_codons)
    return jnp.where(allowed[None], scores, NEG_FILL)


def split_blocks(queries, segments, valid_codons, block_rows):
    block_count = queries.shape[0] // block_rows
    starts = jnp.arange(block_count, dtype=jnp.int32) * block_rows
    return (
        queries.reshape(block_count, block_rows, HEADS, HEAD_DIM),
        segments.reshape(block_count, block_rows),
        valid_codons.reshape(block_count, block_rows),
        starts,
    )


def attend_forward(queries, key_rows, value_rows, segments, valid_codons, block_rows):
    length = queries.shape[0]

    def one_block(running, block_item):
        block_queries, block_segments, block_valid, block_start = block_item
        scores = block_scores(
            block_queries,
            key_rows,
            block_segments,
            block_valid,
            block_start,
            segments,
            valid_codons,
        )
        row_peak = jnp.max(scores, -1, keepdims=True)
        shifted = jnp.exp(scores - row_peak)
        row_total = jnp.sum(shifted, -1, keepdims=True)
        weights = (shifted / row_total).astype(jnp.bfloat16)
        attended = jnp.einsum(
            "hqk,khd->qhd", weights, value_rows, preferred_element_type=jnp.float32
        )
        log_total = (row_peak + jnp.log(row_total))[..., 0]
        return (running, (attended, log_total))

    ignored, (attended, log_total) = lax.scan(
        one_block,
        jnp.zeros((), jnp.float32),
        split_blocks(queries, segments, valid_codons, block_rows),
    )
    return (attended.reshape(length, HEADS, HEAD_DIM), log_total)


def attend_backward(
    queries, key_rows, value_rows, attended_grad, log_total, segments, valid_codons, block_rows
):
    length = queries.shape[0]
    block_queries_all, block_segments_all, block_valid_all, starts = split_blocks(
        queries, segments, valid_codons, block_rows
    )
    grad_blocks = attended_grad.reshape(block_queries_all.shape)
    score_scale = 1.0 / math.sqrt(HEAD_DIM)

    def one_block(running, block_item):
        key_grad, value_grad = running
        block_queries, block_grad, block_log, block_segments, block_valid, block_start = block_item
        scores = block_scores(
            block_queries,
            key_rows,
            block_segments,
            block_valid,
            block_start,
            segments,
            valid_codons,
        )
        weights = jnp.exp(scores - block_log[..., None])
        weight_grad = jnp.einsum(
            "qhd,khd->hqk", block_grad, value_rows, preferred_element_type=jnp.float32
        )
        row_dot = jnp.sum(weights * weight_grad, -1, keepdims=True)
        score_grad = (weights * (weight_grad - row_dot)).astype(jnp.bfloat16)
        query_grad = (
            jnp.einsum("hqk,khd->qhd", score_grad, key_rows, preferred_element_type=jnp.float32)
            * score_scale
        )
        key_grad = (
            key_grad
            + jnp.einsum(
                "hqk,qhd->khd", score_grad, block_queries, preferred_element_type=jnp.float32
            )
            * score_scale
        )
        value_grad = value_grad + jnp.einsum(
            "hqk,qhd->khd",
            weights.astype(jnp.bfloat16),
            block_grad,
            preferred_element_type=jnp.float32,
        )
        return ((key_grad, value_grad), query_grad)

    zero_grad = jnp.zeros(key_rows.shape, jnp.float32)
    scanned = (
        block_queries_all,
        grad_blocks,
        log_total,
        block_segments_all,
        block_valid_all,
        starts,
    )
    (key_grad, value_grad), query_grad = lax.scan(one_block, (zero_grad, zero_grad), scanned)
    return (query_grad.reshape(length, HEADS, HEAD_DIM), key_grad, value_grad)


def body(
    layer_input,
    cotangent,
    segment_ids,
    pad_mask,
    ln1_gain,
    ln1_bias,
    w_qkv,
    b_qkv,
    w_out,
    b_out,
    ln2_gain,
    ln2_bias,
    w_up,
    b_up,
    w_down,
    b_down,
):
    gain_one, bias_one, qkv_weight, qkv_bias, out_weight, out_bias = (
        lax.all_gather(ln1_gain, "fsdp", axis=0, tiled=True),
        lax.all_gather(ln1_bias, "fsdp", axis=0, tiled=True),
        lax.all_gather(w_qkv, "fsdp", axis=0, tiled=True),
        lax.all_gather(b_qkv, "fsdp", axis=0, tiled=True),
        lax.all_gather(w_out, "fsdp", axis=0, tiled=True),
        lax.all_gather(b_out, "fsdp", axis=0, tiled=True),
    )
    gain_two, bias_two, up_weight, up_bias, down_weight, down_bias = (
        lax.all_gather(ln2_gain, "fsdp", axis=0, tiled=True),
        lax.all_gather(ln2_bias, "fsdp", axis=0, tiled=True),
        lax.all_gather(w_up, "fsdp", axis=0, tiled=True),
        lax.all_gather(b_up, "fsdp", axis=0, tiled=True),
        lax.all_gather(w_down, "fsdp", axis=0, tiled=True),
        lax.all_gather(b_down, "fsdp", axis=0, tiled=True),
    )
    length = layer_input.shape[1]
    model_width = layer_input.shape[2]
    block_rows = min(512, length)
    segments = segment_ids[0]
    valid_codons = pad_mask[0]
    cosine_table, sine_table = rotary_tables(gene_positions(segments))
    inputs = layer_input[0].astype(jnp.float32)
    normed, norm_one_back = jax.vjp(
        layer_norm, inputs, gain_one.astype(jnp.float32), bias_one.astype(jnp.float32)
    )
    normed = normed.astype(jnp.bfloat16)
    projected = jnp.dot(normed, qkv_weight, preferred_element_type=jnp.float32) + qkv_bias.astype(
        jnp.float32
    )
    head_shape = (length, HEADS, HEAD_DIM)
    queries = rotate(
        projected[:, :model_width].reshape(head_shape), cosine_table, sine_table
    ).astype(jnp.bfloat16)
    key_rows = rotate(
        projected[:, model_width : 2 * model_width].reshape(head_shape), cosine_table, sine_table
    ).astype(jnp.bfloat16)
    value_rows = projected[:, 2 * model_width :].reshape(head_shape).astype(jnp.bfloat16)
    attended, log_total = attend_forward(
        queries, key_rows, value_rows, segments, valid_codons, block_rows
    )
    attended = attended.reshape(length, model_width).astype(jnp.bfloat16)
    middle = (
        inputs
        + jnp.dot(attended, out_weight, preferred_element_type=jnp.float32)
        + out_bias.astype(jnp.float32)
    )
    normed_two, norm_two_back = jax.vjp(
        layer_norm, middle, gain_two.astype(jnp.float32), bias_two.astype(jnp.float32)
    )
    normed_two = normed_two.astype(jnp.bfloat16)
    hidden = jnp.dot(normed_two, up_weight, preferred_element_type=jnp.float32) + up_bias.astype(
        jnp.float32
    )
    activated, gelu_back = jax.vjp(exact_gelu, hidden)
    activated = activated.astype(jnp.bfloat16)
    layer_out = (
        middle
        + jnp.dot(activated, down_weight, preferred_element_type=jnp.float32)
        + down_bias.astype(jnp.float32)
    ).astype(jnp.bfloat16)
    up_weight_back, down_weight_back = (
        lax.all_gather(w_up, "fsdp", axis=0, tiled=True),
        lax.all_gather(w_down, "fsdp", axis=0, tiled=True),
    )
    out_grad_rows = cotangent[0]
    grad_down_bias = jnp.sum(out_grad_rows.astype(jnp.float32), 0)
    (hidden_grad,) = gelu_back(times_transpose(out_grad_rows, down_weight_back))
    hidden_grad = hidden_grad.astype(jnp.bfloat16)
    grad_up_bias = jnp.sum(hidden_grad.astype(jnp.float32), 0)
    middle_grad, grad_gain_two, grad_bias_two = norm_two_back(
        times_transpose(hidden_grad, up_weight_back)
    )
    middle_grad = middle_grad + out_grad_rows.astype(jnp.float32)
    grad_up_weight = contract_rows(normed_two, hidden_grad)
    grad_down_weight = contract_rows(activated, out_grad_rows)
    ffn_sums = (
        lax.psum_scatter(grad_gain_two, "fsdp", scatter_dimension=0, tiled=True),
        lax.psum_scatter(grad_bias_two, "fsdp", scatter_dimension=0, tiled=True),
        lax.psum_scatter(grad_up_weight, "fsdp", scatter_dimension=0, tiled=True),
        lax.psum_scatter(grad_up_bias, "fsdp", scatter_dimension=0, tiled=True),
        lax.psum_scatter(grad_down_weight, "fsdp", scatter_dimension=0, tiled=True),
        lax.psum_scatter(grad_down_bias, "fsdp", scatter_dimension=0, tiled=True),
    )
    qkv_weight_back, out_weight_back = (
        lax.all_gather(w_qkv, "fsdp", axis=0, tiled=True),
        lax.all_gather(w_out, "fsdp", axis=0, tiled=True),
    )
    branch_grad = middle_grad.astype(jnp.bfloat16)
    grad_out_bias = jnp.sum(branch_grad.astype(jnp.float32), 0)
    attended_grad = (
        times_transpose(branch_grad, out_weight_back).astype(jnp.bfloat16).reshape(head_shape)
    )
    query_grad, key_grad, value_grad = attend_backward(
        queries, key_rows, value_rows, attended_grad, log_total, segments, valid_codons, block_rows
    )
    projected_grad = jnp.concatenate(
        [
            rotate(query_grad, cosine_table, -sine_table).reshape(length, model_width),
            rotate(key_grad, cosine_table, -sine_table).reshape(length, model_width),
            value_grad.reshape(length, model_width),
        ],
        1,
    ).astype(jnp.bfloat16)
    grad_qkv_bias = jnp.sum(projected_grad.astype(jnp.float32), 0)
    input_part, grad_gain_one, grad_bias_one = norm_one_back(
        times_transpose(projected_grad, qkv_weight_back)
    )
    input_grad = (middle_grad + input_part).astype(jnp.bfloat16)
    grad_out_weight = contract_rows(attended, branch_grad)
    grad_qkv_weight = contract_rows(normed, projected_grad)
    attn_sums = (
        lax.psum_scatter(grad_gain_one, "fsdp", scatter_dimension=0, tiled=True),
        lax.psum_scatter(grad_bias_one, "fsdp", scatter_dimension=0, tiled=True),
        lax.psum_scatter(grad_qkv_weight, "fsdp", scatter_dimension=0, tiled=True),
        lax.psum_scatter(grad_qkv_bias, "fsdp", scatter_dimension=0, tiled=True),
        lax.psum_scatter(grad_out_weight, "fsdp", scatter_dimension=0, tiled=True),
        lax.psum_scatter(grad_out_bias, "fsdp", scatter_dimension=0, tiled=True),
    )
    reduced = (
        lax.psum(attn_sums[0].astype(jnp.bfloat16), "replica").astype(jnp.float32),
        lax.psum(attn_sums[1].astype(jnp.bfloat16), "replica").astype(jnp.float32),
        lax.psum(attn_sums[2].astype(jnp.bfloat16), "replica").astype(jnp.float32),
        lax.psum(attn_sums[3].astype(jnp.bfloat16), "replica").astype(jnp.float32),
        lax.psum(attn_sums[4].astype(jnp.bfloat16), "replica").astype(jnp.float32),
        lax.psum(attn_sums[5].astype(jnp.bfloat16), "replica").astype(jnp.float32),
        lax.psum(ffn_sums[0].astype(jnp.bfloat16), "replica").astype(jnp.float32),
        lax.psum(ffn_sums[1].astype(jnp.bfloat16), "replica").astype(jnp.float32),
        lax.psum(ffn_sums[2].astype(jnp.bfloat16), "replica").astype(jnp.float32),
        lax.psum(ffn_sums[3].astype(jnp.bfloat16), "replica").astype(jnp.float32),
        lax.psum(ffn_sums[4].astype(jnp.bfloat16), "replica").astype(jnp.float32),
        lax.psum(ffn_sums[5].astype(jnp.bfloat16), "replica").astype(jnp.float32),
    )
    return (
        layer_out[None],
        input_grad[None],
        reduced[0],
        reduced[1],
        reduced[2],
        reduced[3],
        reduced[4],
        reduced[5],
        reduced[6],
        reduced[7],
        reduced[8],
        reduced[9],
        reduced[10],
        reduced[11],
    )


def solution(mesh):
    in_specs = (
        P(("fsdp", "replica"), None, None),
        P(("fsdp", "replica"), None, None),
        P(("fsdp", "replica"), None),
        P(("fsdp", "replica"), None),
        P("fsdp"),
        P("fsdp"),
        P("fsdp", None),
        P("fsdp"),
        P("fsdp", None),
        P("fsdp"),
        P("fsdp"),
        P("fsdp"),
        P("fsdp", None),
        P("fsdp"),
        P("fsdp", None),
        P("fsdp"),
    )
    out_specs = (
        P(("fsdp", "replica"), None, None),
        P(("fsdp", "replica"), None, None),
        P("fsdp"),
        P("fsdp"),
        P("fsdp", None),
        P("fsdp"),
        P("fsdp", None),
        P("fsdp"),
        P("fsdp"),
        P("fsdp"),
        P("fsdp", None),
        P("fsdp"),
        P("fsdp", None),
        P("fsdp"),
    )
    return jax.shard_map(body, mesh=mesh, in_specs=in_specs, out_specs=out_specs, check_vma=False)
```

profile of v0, /device:TPU:0, one launch (start us, length us, event | category | flops | bytes accessed | tf_op | source)
XLA Modules:
  0.0 1118.5 jit_solution(7735304638543786908)
XLA Ops:
  24.4 39.9 %all-reduce.16 = (bf16[768]{0:T(1024)(128)(2,1)}, bf16[2304]{0:T(1024)(128)(2,1)S(1)}, bf16[768]{0:T(1024)(128)(2,1)S(1)}, bf16[768]{0:T(1024)(128)(2,1)S(1)}, b...) all-reduce(bf16[768]{0:T(1024)(128)(2,1)S(1)} %dynamic-update-slice, ...), channel_id=1, replica_groups=mesh['fsdp'=8,'replica'=4] {'fsdp'}, use_global_device_ids=true, to_apply=%add.6 | all-reduce | flops 6912 | bytes 27648
  66.0 25.9 %all-gather = bf16[8,1,384]{2,1,0:T(2,128)(2,1)S(1)} all-gather(bf16[1,1,384]{2,1,0:T(2,128)(2,1)S(1)} %reshape.495), channel_id=1, replica_groups=mesh['fsdp'=8,'replica'=4] {'fsdp'}, dimensions={0}, use_global_device_ids=true | all-gather | bytes 6912 | tf_op jit(solution)/shard_map/all_gather | solution.py:218
  121.5 74.1 %while.27 = (s32[]{:T(128)}, bf16[2,512,12,64]{1,3,2,0:T(8,128)(2,1)}, f32[2,12,512]{2,1,0:T(8,128)S(1)}, s32[2,512]{1,0:T(2,128)S(1)}, s32[1,1024]{1,0:T(1,128)...) while((s32[]{:T(128)}, ...), condition=%wide.region_8.9_spmd, body=%wide.region_5.8_spmd.sunk | while | flops 1688727552 | bytes 190299344 | solution.py:120
  123.7 11.0 fusion.120
  134.7 12.4 %fusion.121 = f32[12,512]{1,0:T(8,128)S(1)} fusion(f32[12,512,1024]{2,1,0:T(8,128)} %get-tuple-element.584, f32[12,512]{1,0:T(8,128)S(1)} %get-tuple-element.585, pred[512,1024]{1,0:T(8,128)(4,1)S(1)} %fusion.119), kind=kLoop, calls=%fused_computation.4.clone.1 | loop fusion | flops 25159680 | bytes 25739264 | tf_op jit(solution)/shard_map/while/body/eval_jaxpr/reduce_sum | solution.py:112
  160.8 10.7 fusion.120
  171.5 12.3 %fusion.121 = f32[12,512]{1,0:T(8,128)S(1)} fusion(f32[12,512,1024]{2,1,0:T(8,128)} %get-tuple-element.584, f32[12,512]{1,0:T(8,128)S(1)} %get-tuple-element.585, pred[512,1024]{1,0:T(8,128)(4,1)S(1)} %fusion.119), kind=kLoop, calls=%fused_computation.4.clone.1 | loop fusion | flops 25159680 | bytes 25739264 | tf_op jit(solution)/shard_map/while/body/eval_jaxpr/reduce_sum | solution.py:112
  206.1 37.9 %multiply_convert_fusion.1 = (bf16[1024,3072]{1,0:T(8,128)(2,1)}, f32[1024,3072]{1,0:T(8,128)}, f32[1024,3072]{1,0:T(8,128)}) fusion(f32[3072]{0:T(1024)S(1)} %bitcast.217, bf16[768,3072]{1,0:T(8,128)(2,1)} %all-gather.10.cloned.1.call-done, f32[1024,768]{0,1:T(8,128)S(1)} %get-tuple-element.432, f32[768]{0:T(1024)S(1)} %copy-done.60, ...), kind=kOutput, calls=%fused_computation.56 | convolution fusion | flops 5043388416 | bytes 39348224 | tf_op jit(solution)/shard_map/dot_general | solution.py:257
  244.0 37.8 %all-gather.12.cloned.1.call-done = bf16[3072,768]{1,0:T(8,128)(2,1)} async-done(((bf16[384,768]{1,0:T(8,128)(2,1)}), bf16[3072,768]{1,0:T(8,128)(2,1)}) %all-gather.12.cloned.1.call-update) | async-done | bytes 4718608 | tf_op jit(solution)/shard_map/all_gather | solution.py:219
  281.8 19.1 %convert_reduce_fusion = (f32[3072]{0:T(1024)}, bf16[1024,3072]{1,0:T(8,128)(2,1)}) fusion(f32[1024,3072]{1,0:T(8,128)} %get-tuple-element.405, bf16[3072,768]{1,0:T(8,128)(2,1)} %all-gather.12.cloned.1.call-done, bf16[1,1024,768]{2,1,0:T(8,128)(2,1)} %param.21, f32[1024,3072]{1,0:T(8,128)} %get-tuple-element.433, f32[3072]{0:T(1024)S(1)} %bitcast.218), kind=kOutput, calls=%fused_computation.54 | convolution fusion | flops 4885312512 | bytes 37773312 | tf_op jit(solution)/shard_map/dot_general | solution.py:21
  300.9 10.4 fusion.76
  331.0 233.6 %while.28 = (s32[]{:T(128)}, f32[1024,12,64]{0,2,1:T(8,128)}, f32[1024,12,64]{0,2,1:T(8,128)}, f32[2,512,12,64]{1,0,3,2:T(2,128)}, bf16[2,512,12,64]{1,3,2,0:T(8...) while((s32[]{:T(128)}, f32[1024,12,64]{0,2,1:T(8,128)}, ...), condition=%wide.region_15.16_spmd.clone, body=%wide.region_13.15_spmd.clone.sunk | while | flops 4127846400 | bytes 238230832 | solution.py:184
  333.2 11.4 %fusion.131 = f32[12,512,1024]{2,1,0:T(8,128)} fusion(bf16[1024,12,64]{0,2,1:T(8,128)(2,1)S(1)} %get-tuple-element.680, bf16[2,512,12,64]{1,3,2,0:T(8,128)(2,1)} %get-tuple-element.674, s32[]{:T(128)S(6)} %copy.152), kind=kOutput, calls=%fused_computation.35.clone.1 | convolution fusion | flops 805306368 | bytes 27525124 | tf_op jit(solution)/shard_map/while/body/eval_jaxpr/qhd,khd->hqk/dot_general | solution.py:78
  344.7 13.8 %bitcast_add_fusion.5 = f32[1024,12,64]{0,2,1:T(8,128)} fusion(f32[1024,12,64]{0,2,1:T(8,128)} %get-tuple-element.656, f32[12,512,1024]{2,1,0:T(8,128)} %fusion.131, f32[12,512]{1,0:T(8,128)S(1)} %dynamic-slice_bitcast_fusion.2, pred[512,1024]{1,0:T(8,128)(4,1)S(1)} %fusion.132, pred[]{:T(512)S(6)} %compare.3, ...), kind=kOutput, calls=%fused_computation.26.clone.1 | convolution fusion | flops 832045056 | bytes 32800772 | tf_op jit(solution)/shard_map/while/body/eval_jaxpr/hqk,qhd->khd/dot_general | solution.py:167
  358.5 18.2 %multiply_reduce_fusion.5 = (f32[12,512]{1,0:T(8,128)S(1)}, f32[12,512,1024]{2,1,0:T(8,128)}) fusion(f32[12,512,1024]{2,1,0:T(8,128)} %fusion.131, f32[12,512]{1,0:T(8,128)S(1)} %dynamic-slice_bitcast_fusion.2, pred[512,1024]{1,0:T(8,128)(4,1)S(1)} %fusion.132, bf16[1024,12,64]{0,2,1:T(8,128)(2,1)} %get-tuple-element.683, ...), kind=kOutput, calls=%fused_computation.21.clone.1 | convolution fusion | flops 836757504 | bytes 53264388 | tf_op jit(solution)/shard_map/while/body/eval_jaxpr/qhd,khd->hqk/dot_general | solution.py:151
  376.7 21.7 %multiply_convert_fusion.3 = bf16[12,512,1024]{2,1,0:T(8,128)(2,1)} fusion(f32[12,512,1024]{2,1,0:T(8,128)} %get-tuple-element.600, f32[12,512,1024]{2,1,0:T(8,128)} %fusion.131, f32[12,512]{1,0:T(8,128)S(1)} %get-tuple-element.601, f32[12,512]{1,0:T(8,128)S(1)} %dynamic-slice_bitcast_fusion.2, pred[512,1024]{1,0:T(8,128)(4,1)S(1)} %fusion.132), kind=kLoop, calls=%fused_computation.20.clone.1 | loop fusion | flops 37748736 | bytes 63488000 | tf_op jit(solution)/shard_map/while/body/eval_jaxpr/convert_element_type | solution.py:155
  398.4 9.8 multiply_bitcast_fusion.2
  418.6 28.8 %dynamic_update_slice.19 = f32[2,512,12,64]{1,0,3,2:T(2,128)} dynamic-update-slice(f32[2,512,12,64]{1,0,3,2:T(2,128)} %get-tuple-element.657, f32[1,512,12,64]{1,0,3,2:T(1,128)S(1)} %copy.127, s32[]{:T(128)S(6)} %copy.152, s32[]{:T(128)} %constant.33.clone.1..sunk, s32[]{:T(128)} %constant.33.clone.1..sunk, s32[]{:T(128)} %constant.33.clone.1..sunk) | dynamic-update-slice | bytes 3145732 | tf_op jit(solution)/shard_map/while/body/jit(dynamic_update_index_in_dim)/dynamic_update_slice | solution.py:120
  449.4 11.4 %fusion.131 = f32[12,512,1024]{2,1,0:T(8,128)} fusion(bf16[1024,12,64]{0,2,1:T(8,128)(2,1)S(1)} %get-tuple-element.680, bf16[2,512,12,64]{1,3,2,0:T(8,128)(2,1)} %get-tuple-element.674, s32[]{:T(128)S(6)} %copy.152), kind=kOutput, calls=%fused_computation.35.clone.1 | convolution fusion | flops 805306368 | bytes 27525124 | tf_op jit(solution)/shard_map/while/body/eval_jaxpr/qhd,khd->hqk/dot_general | solution.py:78
  460.8 14.3 %bitcast_add_fusion.5 = f32[1024,12,64]{0,2,1:T(8,128)} fusion(f32[1024,12,64]{0,2,1:T(8,128)} %get-tuple-element.656, f32[12,512,1024]{2,1,0:T(8,128)} %fusion.131, f32[12,512]{1,0:T(8,128)S(1)} %dynamic-slice_bitcast_fusion.2, pred[512,1024]{1,0:T(8,128)(4,1)S(1)} %fusion.132, pred[]{:T(512)S(6)} %compare.3, ...), kind=kOutput, calls=%fused_computation.26.clone.1 | convolution fusion | flops 832045056 | bytes 32800772 | tf_op jit(solution)/shard_map/while/body/eval_jaxpr/hqk,qhd->khd/dot_general | solution.py:167
  475.1 18.1 %multiply_reduce_fusion.5 = (f32[12,512]{1,0:T(8,128)S(1)}, f32[12,512,1024]{2,1,0:T(8,128)}) fusion(f32[12,512,1024]{2,1,0:T(8,128)} %fusion.131, f32[12,512]{1,0:T(8,128)S(1)} %dynamic-slice_bitcast_fusion.2, pred[512,1024]{1,0:T(8,128)(4,1)S(1)} %fusion.132, bf16[1024,12,64]{0,2,1:T(8,128)(2,1)} %get-tuple-element.683, ...), kind=kOutput, calls=%fused_computation.21.clone.1 | convolution fusion | flops 836757504 | bytes 53264388 | tf_op jit(solution)/shard_map/while/body/eval_jaxpr/qhd,khd->hqk/dot_general | solution.py:151
  493.2 21.2 %multiply_convert_fusion.3 = bf16[12,512,1024]{2,1,0:T(8,128)(2,1)} fusion(f32[12,512,1024]{2,1,0:T(8,128)} %get-tuple-element.600, f32[12,512,1024]{2,1,0:T(8,128)} %fusion.131, f32[12,512]{1,0:T(8,128)S(1)} %get-tuple-element.601, f32[12,512]{1,0:T(8,128)S(1)} %dynamic-slice_bitcast_fusion.2, pred[512,1024]{1,0:T(8,128)(4,1)S(1)} %fusion.132), kind=kLoop, calls=%fused_computation.20.clone.1 | loop fusion | flops 37748736 | bytes 63488000 | tf_op jit(solution)/shard_map/while/body/eval_jaxpr/convert_element_type | solution.py:155
  514.4 9.8 multiply_bitcast_fusion.2
  524.2 9.6 bitcast_add_fusion.4
  535.4 28.8 %dynamic_update_slice.19 = f32[2,512,12,64]{1,0,3,2:T(2,128)} dynamic-update-slice(f32[2,512,12,64]{1,0,3,2:T(2,128)} %get-tuple-element.657, f32[1,512,12,64]{1,0,3,2:T(1,128)S(1)} %copy.127, s32[]{:T(128)S(6)} %copy.152, s32[]{:T(128)} %constant.33.clone.1..sunk, s32[]{:T(128)} %constant.33.clone.1..sunk, s32[]{:T(128)} %constant.33.clone.1..sunk) | dynamic-update-slice | bytes 3145732 | tf_op jit(solution)/shard_map/while/body/jit(dynamic_update_index_in_dim)/dynamic_update_slice | solution.py:120
  582.5 10.5 fusion.67
  594.4 10.2 fusion.55
  624.0 9.5 fusion.58
  635.1 74.5 %reduce-scatter.5.cloned.1.call-done = f32[96,2304]{1,0:T(8,128)} async-done(((f32[768,2304]{1,0:T(8,128)}), f32[96,2304]{1,0:T(8,128)}) %reduce-scatter.5.cloned.1.call-update) | async-done | bytes 884752 | tf_op jit(solution)/shard_map/reduce_scatter | solution.py:320
  711.6 164.6 %reduce-scatter.9.cloned.1.call-done = f32[96,3072]{1,0:T(8,128)} async-done(((f32[768,3072]{1,0:T(8,128)}), f32[96,3072]{1,0:T(8,128)}) %reduce-scatter.9.cloned.1.call-update) | async-done | bytes 1179664 | tf_op jit(solution)/shard_map/reduce_scatter | solution.py:285
  878.3 164.5 %reduce-scatter.11.cloned.1.call-done = f32[384,768]{1,0:T(8,128)} async-done(((f32[3072,768]{1,0:T(8,128)}), f32[384,768]{1,0:T(8,128)}) %reduce-scatter.11.cloned.1.call-update) | async-done | bytes 1179664 | tf_op jit(solution)/shard_map/reduce_scatter | solution.py:287
  1056.4 35.3 %all-reduce.15 = (bf16[768]{0:T(1024)(128)(2,1)S(1)}, bf16[768]{0:T(1024)(128)(2,1)S(1)}, bf16[2304]{0:T(1024)(128)(2,1)S(1)}, bf16[768]{0:T(1024)(128)(2,1)S(1)...) all-reduce(f32[768]{0:T(1024)S(1)} %get-tuple-element.321, ...), channel_id=2, replica_groups=mesh['fsdp'=8,'replica'=4] {'fsdp'}, use_global_device_ids=true, to_apply=%region_19.20.clone | all-reduce | flops 9984 | bytes 59904
  (317 shorter events, 195.7 us)
Async XLA Ops:
  7.2 91.5 %all-gather.6.cloned.1.call-start = ((), (), s32[]{:S(2)}) async-start(), calls=%async_computation.4 | async-start | bytes 3981312 | tf_op jit(solution)/shard_map/all_gather | solution.py:209
  7.9 193.5 %all-gather.8.cloned.1.call-start = ((), (), s32[]{:S(2)}) async-start(), calls=%async_computation.5 | async-start | bytes 1327104 | tf_op jit(solution)/shard_map/all_gather | solution.py:211
  8.7 197.1 %all-gather.10.cloned.1.call-start = ((), (), s32[]{:S(2)}) async-start(), calls=%async_computation.6 | async-start | bytes 5308416 | tf_op jit(solution)/shard_map/all_gather | solution.py:217
  9.4 272.4 %all-gather.12.cloned.1.call-start = ((), (), s32[]{:S(2)}) async-start(), calls=%async_computation.7 | async-start | bytes 5308416 | tf_op jit(solution)/shard_map/all_gather | solution.py:219
  10.0 623.5 %reduce-scatter.7.cloned.1.call-start = ((), (), s32[]{:S(2)}) async-start(), calls=%async_computation.9 | async-start | bytes 2654208 | tf_op jit(solution)/shard_map/reduce_scatter | solution.py:322
  64.2 34.4 %copy-start.41 = (f32[768]{0:T(1024)}, f32[768]{0:T(1024)S(1)}, u32[]{:S(2)}) copy-start(f32[768]{0:T(1024)S(1)} %convert_element_type.174) | copy-start | bytes 9220
  64.8 33.8 %copy-start.62 = (f32[768]{0:T(1024)}, f32[768]{0:T(1024)S(1)}, u32[]{:S(2)}) copy-start(f32[768]{0:T(1024)S(1)} %convert_element_type.175) | copy-start | bytes 9220
  94.7 10.3 copy-start.39
  95.8 9.2 copy-start.45
  98.6 19.3 %copy-start.25 = (f32[1024,32]{0,1:T(8,128)}, f32[1024,32]{0,1:T(8,128)S(1)}, u32[]{:S(2)}) copy-start(f32[1024,32]{0,1:T(8,128)S(1)} %get-tuple-element.428) | copy-start | bytes 393220
  123.7 23.4 %copy-start.7 = (bf16[1024,12,64]{0,2,1:T(8,128)(2,1)S(1)}, bf16[1024,12,64]{0,2,1:T(8,128)(2,1)}, u32[]{:S(2)}) copy-start(bf16[1024,12,64]{0,2,1:T(8,128)(2,1)} %get-tuple-element.636) | copy-start | bytes 4718596 | tf_op jit(solution)/shard_map/while
  134.7 15.6 %copy-start = (f32[12,512,1024]{2,1,0:T(8,128)S(1)}, f32[12,512,1024]{2,1,0:T(8,128)}, u32[]{:S(2)}) copy-start(f32[12,512,1024]{2,1,0:T(8,128)} %get-tuple-element.584) | copy-start | bytes 75497472 | tf_op jit(solution)/shard_map/while
  160.8 23.0 %copy-start.7 = (bf16[1024,12,64]{0,2,1:T(8,128)(2,1)S(1)}, bf16[1024,12,64]{0,2,1:T(8,128)(2,1)}, u32[]{:S(2)}) copy-start(bf16[1024,12,64]{0,2,1:T(8,128)(2,1)} %get-tuple-element.636) | copy-start | bytes 4718596 | tf_op jit(solution)/shard_map/while
  171.5 15.6 %copy-start = (f32[12,512,1024]{2,1,0:T(8,128)S(1)}, f32[12,512,1024]{2,1,0:T(8,128)}, u32[]{:S(2)}) copy-start(f32[12,512,1024]{2,1,0:T(8,128)} %get-tuple-element.584) | copy-start | bytes 75497472 | tf_op jit(solution)/shard_map/while
  205.3 113.1 %copy-start.12 = (f32[1024,768]{0,1:T(8,128)}, f32[1024,768]{0,1:T(8,128)S(1)}, u32[]{:S(2)}) copy-start(f32[1024,768]{0,1:T(8,128)S(1)} %get-tuple-element.432) | copy-start | bytes 9437188
  205.3 113.0 %copy-start.43 = (f32[1024]{0:T(1024)}, f32[1024]{0:T(1024)S(1)}, u32[]{:S(2)}) copy-start(f32[1024]{0:T(1024)S(1)} %broadcast_multiply_fusion) | copy-start | bytes 12292
  205.8 112.6 %copy-start.53 = (f32[1024]{0:T(1024)}, f32[1024]{0:T(1024)S(1)}, u32[]{:S(2)}) copy-start(f32[1024]{0:T(1024)S(1)} %fusion.62) | copy-start | bytes 12292
  330.9 378.7 %reduce-scatter.5.cloned.1.call-start = ((), (), s32[]{:S(2)}) async-start(), calls=%async_computation.8 | async-start | bytes 7962624 | tf_op jit(solution)/shard_map/reduce_scatter | solution.py:320
  333.2 11.4 %copy-start.15 = (bf16[2,512,12,64]{1,3,2,0:T(8,128)(2,1)S(1)}, bf16[2,512,12,64]{1,3,2,0:T(8,128)(2,1)}, u32[]{:S(2)}) copy-start(bf16[2,512,12,64]{1,3,2,0:T(8,128)(2,1)} %get-tuple-element.682) | copy-start | bytes 4718596 | tf_op jit(solution)/shard_map/while
  398.4 9.8 copy-start.6
  408.2 8.7 copy-start.4
  449.4 11.4 %copy-start.15 = (bf16[2,512,12,64]{1,3,2,0:T(8,128)(2,1)S(1)}, bf16[2,512,12,64]{1,3,2,0:T(8,128)(2,1)}, u32[]{:S(2)}) copy-start(bf16[2,512,12,64]{1,3,2,0:T(8,128)(2,1)} %get-tuple-element.682) | copy-start | bytes 4718596 | tf_op jit(solution)/shard_map/while
  514.4 9.8 copy-start.6
  524.2 9.6 copy-start.4
  581.8 294.4 %reduce-scatter.9.cloned.1.call-start = ((), (), s32[]{:S(2)}) async-start(), calls=%async_computation.10 | async-start | bytes 10616832 | tf_op jit(solution)/shard_map/reduce_scatter | solution.py:285
  593.0 449.8 %reduce-scatter.11.cloned.1.call-start = ((), (), s32[]{:S(2)}) async-start(), calls=%async_computation.11 | async-start | bytes 10616832 | tf_op jit(solution)/shard_map/reduce_scatter | solution.py:287
  604.7 500.2 %all-reduce.21.cloned.1.call-start = ((), (), s32[]{:S(2)}) async-start(), calls=%async_computation.12 | async-start | bytes 3538944 | tf_op jit(solution)/shard_map/psum | solution.py:328
  1050.4 5.9 copy-start.55
  1050.4 5.9 copy-start.56
  1050.4 5.9 copy-start.58
  1050.5 5.9 copy-start.59
  1104.9 5.9 copy-start.29
  (50 other events, 124.4 us)
Sparse Core Ops, SparseCore 0:
  10.2 68.4 all-gather.5
  80.9 39.8 all-gather.7
  123.0 78.6 all-gather.9
  203.8 78.0 all-gather.11
  331.0 67.1 reduce-scatter.6
  582.0 127.5 reduce-scatter.4
  713.6 162.5 reduce-scatter.8
  880.2 162.5 reduce-scatter.10
  1046.8 45.7 all-reduce.20
where the time goes:
time: 1130 us; the launch traced here: 1120 us
  waiting for transfers between devices  444 us (39%)
  matrix products  293 us (26%)
  local copies, waits for them, and re-layouts  129 us (11%)
  other arithmetic  127 us (11%)
  blocking collectives  107 us (9%)
  between operations  18.4 us (2%)
    reduce_scatter x1, waiting for transfers between devices, body(): lax.psum_scatter(grad_up_weight, 'fsdp', scatter_dimension=0, tiled=True)  165 us
    reduce_scatter x1, waiting for transfers between devices, body(): lax.psum_scatter(grad_down_weight, 'fsdp', scatter_dimension=0, tiled=True)  164 us
    unnamed x2, blocking collectives  75.2 us
    reduce_scatter x1, waiting for transfers between devices, body(): lax.psum_scatter(grad_qkv_weight, 'fsdp', scatter_dimension=0, tiled=True)  74.5 us
    dynamic_update_slice x4, local copies, waits for them, and re-layouts, attend_forward(): lax.scan(one_block, jnp.zeros((), jnp.float32), split_blocks(queries, seg...  60.9 us
    dot_general x4, matrix products, block_scores(): jnp.einsum('qhd,khd->hqk', block_queries, key_rows, preferred_element_typ...  44.4 us
    convert_element_type x2, other arithmetic, one_block(): score_grad = (weights * (weight_grad - row_dot)).astype(jnp.bfloat16)  43 us
    dot_general x4, matrix products, times_transpose(): lax.dot_general(left_matrix, right_matrix, (((1,), (1,)), ((), ())), pref...  40.8 us
  transfers between devices with their start and end apart: 9, of which 4 were waited for; matrix products, arithmetic and copies ran while one was open for 43% of the time, Pallas kernels for 0%

commit v1 on v0

--- a/solution.py
+++ b/solution.py
@@ -9,6 +9,27 @@
 GENES = 4
 EPSILON = 1e-05
 NEG_FILL = -1000000000.0
+
+
+def collect(array, axis, dim):
+    length, place, rows = (lax.axis_size(axis), lax.axis_index(axis), array.shape[dim])
+    right = [(i, (i + 1) % length) for i in range(length)]
+    left = [(i, (i - 1) % length) for i in range(length)]
+    out = jnp.zeros((*array.shape[:dim], length * rows, *array.shape[dim + 1 :]), array.dtype)
+    out = lax.dynamic_update_slice_in_dim(out, array, place * rows, axis=dim)
+    from_left = from_right = array
+    middle = length // 2
+    for turn in range(1, middle + 1):
+        from_left = lax.ppermute(from_left, axis, right)
+        out = lax.dynamic_update_slice_in_dim(
+            out, from_left, (place - turn) % length * rows, axis=dim
+        )
+        if turn < length - middle:
+            from_right = lax.ppermute(from_right, axis, left)
+            out = lax.dynamic_update_slice_in_dim(
+                out, from_right, (place + turn) % length * rows, axis=dim
+            )
+    return out
 
 
 def contract_rows(left_matrix, right_matrix):
@@ -216,7 +237,7 @@
         lax.all_gather(ln2_bias, "fsdp", axis=0, tiled=True),
         lax.all_gather(w_up, "fsdp", axis=0, tiled=True),
         lax.all_gather(b_up, "fsdp", axis=0, tiled=True),
-        lax.all_gather(w_down, "fsdp", axis=0, tiled=True),
+        collect(w_down, "fsdp", 0),
         lax.all_gather(b_down, "fsdp", axis=0, tiled=True),
     )
     length = layer_input.shape[1]

time: 1130 us -> 1200 us (1.062)
  starting transfers between devices: 0.53 us -> 34 us
  waiting for transfers between devices: 444 us -> 466 us
  local copies, waits for them, and re-layouts: 129 us -> 145 us
    ppermute x0 -> x7, waiting for transfers between devices: none -> 73.5 us  [the longest x4 72 us: collect(): from_left = lax.ppermute(from_left, axis, right)]
    reduce_scatter x1, waiting for transfers between devices: 74.5 us -> 21.7 us  [body(): lax.psum_scatter(grad_qkv_weight, 'fsdp', scatter_dimension=0, tiled=True)]
    ppermute x0 -> x7, starting transfers between devices: none -> 33.6 us  [the longest x3 30.4 us: collect(): from_right = lax.ppermute(from_right, axis, left)]
    unnamed x158 -> x176, local copies, waits for them, and re-layouts: 28.4 us -> 27 us
  transfers between devices with their start and end apart: 9 -> 16, of which waited for: 4 -> 9; matrix products, arithmetic and copies ran while one was open for 43% -> 42% of each run, Pallas kernels for 0% -> 0%
where the time goes in v1:
time: 1200 us; the launch traced here: 1190 us
  waiting for transfers between devices  466 us (39%)
  matrix products  290 us (24%)
  local copies, waits for them, and re-layouts  145 us (12%)
  other arithmetic  125 us (10%)
  blocking collectives  107 us (9%)
  starting transfers between devices  34 us (3%)
  between operations  18.3 us (2%)
    reduce_scatter x1, waiting for transfers between devices, body(): lax.psum_scatter(grad_up_weight, 'fsdp', scatter_dimension=0, tiled=True)  165 us
    reduce_scatter x1, waiting for transfers between devices, body(): lax.psum_scatter(grad_down_weight, 'fsdp', scatter_dimension=0, tiled=True)  164 us
    unnamed x2, blocking collectives  75.3 us
    ppermute x4, waiting for transfers between devices, collect(): from_left = lax.ppermute(from_left, axis, right)  72 us
    dynamic_update_slice x4, local copies, waits for them, and re-layouts, attend_forward(): lax.scan(one_block, jnp.zeros((), jnp.float32), split_blocks(queries, seg...  63.7 us
    dot_general x4, matrix products, block_scores(): jnp.einsum('qhd,khd->hqk', block_queries, key_rows, preferred_element_typ...  45.1 us
    convert_element_type x2, other arithmetic, one_block(): score_grad = (weights * (weight_grad - row_dot)).astype(jnp.bfloat16)  43.3 us
    all_gather x1, waiting for transfers between devices, body(): lax.all_gather(w_down, 'fsdp', axis=0, tiled=True)  38.8 us
  transfers between devices with their start and end apart: 16, of which 9 were waited for; matrix products, arithmetic and copies ran while one was open for 42% of the time, Pallas kernels for 0%

profile of v1, /device:TPU:0, one launch (start us, length us, event | category | flops | bytes accessed | tf_op | source)
XLA Modules:
  0.0 1186.8 jit_solution(7318314022663115308)
XLA Ops:
  18.7 39.6 %all-reduce.16 = (bf16[768]{0:T(1024)(128)(2,1)}, bf16[2304]{0:T(1024)(128)(2,1)S(1)}, bf16[768]{0:T(1024)(128)(2,1)S(1)}, bf16[768]{0:T(1024)(128)(2,1)S(1)}, b...) all-reduce(bf16[768]{0:T(1024)(128)(2,1)S(1)} %dynamic-update-slice, ...), channel_id=1, replica_groups=mesh['fsdp'=8,'replica'=4] {'fsdp'}, use_global_device_ids=true, to_apply=%add.6 | all-reduce | flops 6912 | bytes 27648
  65.0 26.1 %all-gather = bf16[8,1,384]{2,1,0:T(2,128)(2,1)S(1)} all-gather(bf16[1,1,384]{2,1,0:T(2,128)(2,1)S(1)} %reshape.495), channel_id=1, replica_groups=mesh['fsdp'=8,'replica'=4] {'fsdp'}, dimensions={0}, use_global_device_ids=true | all-gather | bytes 6912 | tf_op jit(solution)/shard_map/all_gather | solution.py:239
  120.1 74.2 %while.27 = (s32[]{:T(128)}, bf16[2,512,12,64]{1,3,2,0:T(8,128)(2,1)}, f32[2,12,512]{2,1,0:T(8,128)S(1)}, s32[2,512]{1,0:T(2,128)S(1)}, s32[1,1024]{1,0:T(1,128)...) while((s32[]{:T(128)}, ...), condition=%wide.region_8.9_spmd, body=%wide.region_5.8_spmd.sunk | while | flops 1688727552 | bytes 190299856 | solution.py:141
  122.4 11.0 fusion.120
  133.4 12.4 %fusion.121 = f32[12,512]{1,0:T(8,128)S(1)} fusion(f32[12,512,1024]{2,1,0:T(8,128)} %get-tuple-element.584, f32[12,512]{1,0:T(8,128)S(1)} %get-tuple-element.585, pred[512,1024]{1,0:T(8,128)(4,1)S(1)} %fusion.119), kind=kLoop, calls=%fused_computation.4.clone.1 | loop fusion | flops 25159680 | bytes 25739264 | tf_op jit(solution)/shard_map/while/body/eval_jaxpr/reduce_sum | solution.py:133
  159.6 10.7 fusion.120
  170.3 12.4 %fusion.121 = f32[12,512]{1,0:T(8,128)S(1)} fusion(f32[12,512,1024]{2,1,0:T(8,128)} %get-tuple-element.584, f32[12,512]{1,0:T(8,128)S(1)} %get-tuple-element.585, pred[512,1024]{1,0:T(8,128)(4,1)S(1)} %fusion.119), kind=kLoop, calls=%fused_computation.4.clone.1 | loop fusion | flops 25159680 | bytes 25739264 | tf_op jit(solution)/shard_map/while/body/eval_jaxpr/reduce_sum | solution.py:133
  204.8 38.1 %multiply_convert_fusion.1 = (bf16[1024,3072]{1,0:T(8,128)(2,1)}, f32[1024,3072]{1,0:T(8,128)}, f32[1024,3072]{1,0:T(8,128)}) fusion(f32[3072]{0:T(1024)S(1)} %bitcast.217, bf16[768,3072]{1,0:T(8,128)(2,1)} %all-gather.10.cloned.1.call-done, f32[1024,768]{0,1:T(8,128)S(1)} %get-tuple-element.432, f32[768]{0:T(1024)S(1)} %copy-done.69, ...), kind=kOutput, calls=%fused_computation.56 | convolution fusion | flops 5043388416 | bytes 39348224 | tf_op jit(solution)/shard_map/dot_general | solution.py:278
  242.8 38.8 %all-gather.12.cloned.1.call-done = bf16[3072,768]{1,0:T(8,128)(2,1)} async-done(((bf16[384,768]{1,0:T(8,128)(2,1)}), bf16[3072,768]{1,0:T(8,128)(2,1)}) %all-gather.12.cloned.1.call-update) | async-done | bytes 4718608 | tf_op jit(solution)/shard_map/all_gather | solution.py:290
  281.6 18.9 %convert_reduce_fusion = (f32[3072]{0:T(1024)}, bf16[1024,3072]{1,0:T(8,128)(2,1)}) fusion(f32[1024,3072]{1,0:T(8,128)} %get-tuple-element.405, bf16[3072,768]{1,0:T(8,128)(2,1)} %all-gather.12.cloned.1.call-done, bf16[1,1024,768]{2,1,0:T(8,128)(2,1)} %param.21, f32[1024,3072]{1,0:T(8,128)} %get-tuple-element.433, f32[3072]{0:T(1024)S(1)} %bitcast.218), kind=kOutput, calls=%fused_computation.54 | convolution fusion | flops 4885312512 | bytes 37773312 | tf_op jit(solution)/shard_map/dot_general | solution.py:42
  300.5 10.3 fusion.76
  333.3 237.1 %while.28 = (s32[]{:T(128)}, f32[1024,12,64]{0,2,1:T(8,128)}, f32[1024,12,64]{0,2,1:T(8,128)}, f32[2,512,12,64]{1,0,3,2:T(2,128)}, bf16[2,512,12,64]{1,3,2,0:T(8...) while((s32[]{:T(128)}, f32[1024,12,64]{0,2,1:T(8,128)}, ...), condition=%wide.region_15.16_spmd.clone, body=%wide.region_13.15_spmd.clone.sunk | while | flops 4127846400 | bytes 229843728 | solution.py:205
  335.8 11.8 fusion.131
  347.6 18.2 %multiply_reduce_fusion.5 = (f32[12,512]{1,0:T(8,128)S(1)}, f32[12,512,1024]{2,1,0:T(8,128)}) fusion(f32[12,512,1024]{2,1,0:T(8,128)} %fusion.131, f32[12,512]{1,0:T(8,128)S(1)} %dynamic-slice_bitcast_fusion.2, pred[512,1024]{1,0:T(8,128)(4,1)S(1)} %fusion.132, bf16[1024,12,64]{0,2,1:T(8,128)(2,1)} %get-tuple-element.683, ...), kind=kOutput, calls=%fused_computation.21.clone.1 | convolution fusion | flops 836757504 | bytes 53264896 | tf_op jit(solution)/shard_map/while/body/eval_jaxpr/qhd,khd->hqk/dot_general | solution.py:172
  365.8 22.1 %multiply_convert_fusion.3 = bf16[12,512,1024]{2,1,0:T(8,128)(2,1)} fusion(f32[12,512,1024]{2,1,0:T(8,128)} %get-tuple-element.600, f32[12,512,1024]{2,1,0:T(8,128)} %fusion.131, f32[12,512]{1,0:T(8,128)S(1)} %get-tuple-element.601, f32[12,512]{1,0:T(8,128)S(1)} %dynamic-slice_bitcast_fusion.2, pred[512,1024]{1,0:T(8,128)(4,1)S(1)} %fusion.132), kind=kLoop, calls=%fused_computation.20.clone.1 | loop fusion | flops 37748736 | bytes 63488000 | tf_op jit(solution)/shard_map/while/body/eval_jaxpr/convert_element_type | solution.py:176
  400.7 28.8 %dynamic_update_slice.59 = f32[2,512,12,64]{1,0,3,2:T(2,128)} dynamic-update-slice(f32[2,512,12,64]{1,0,3,2:T(2,128)} %get-tuple-element.657, f32[1,512,12,64]{1,0,3,2:T(1,128)S(1)} %copy.127, s32[]{:T(128)} %get-tuple-element.654, s32[]{:T(128)} %constant.86.clone.1..sunk, s32[]{:T(128)} %constant.86.clone.1..sunk, s32[]{:T(128)} %constant.86.clone.1..sunk) | dynamic-update-slice | bytes 3145732 | tf_op jit(solution)/shard_map/while/body/jit(dynamic_update_index_in_dim)/dynamic_update_slice | solution.py:141
  438.5 13.4 %bitcast_add_fusion.5 = f32[1024,12,64]{0,2,1:T(8,128)} fusion(f32[1024,12,64]{0,2,1:T(8,128)} %get-tuple-element.656, f32[12,512,1024]{2,1,0:T(8,128)} %fusion.131, f32[12,512]{1,0:T(8,128)S(1)} %dynamic-slice_bitcast_fusion.2, pred[512,1024]{1,0:T(8,128)(4,1)S(1)} %copy-done.5, pred[]{:T(512)S(6)} %compare.10, ...), kind=kOutput, calls=%fused_computation.26.clone.1 | convolution fusion | flops 832045056 | bytes 32800772 | tf_op jit(solution)/shard_map/while/body/eval_jaxpr/hqk,qhd->khd/dot_general | solution.py:188
  453.9 11.5 fusion.131
  465.4 18.1 %multiply_reduce_fusion.5 = (f32[12,512]{1,0:T(8,128)S(1)}, f32[12,512,1024]{2,1,0:T(8,128)}) fusion(f32[12,512,1024]{2,1,0:T(8,128)} %fusion.131, f32[12,512]{1,0:T(8,128)S(1)} %dynamic-slice_bitcast_fusion.2, pred[512,1024]{1,0:T(8,128)(4,1)S(1)} %fusion.132, bf16[1024,12,64]{0,2,1:T(8,128)(2,1)} %get-tuple-element.683, ...), kind=kOutput, calls=%fused_computation.21.clone.1 | convolution fusion | flops 836757504 | bytes 53264896 | tf_op jit(solution)/shard_map/while/body/eval_jaxpr/qhd,khd->hqk/dot_general | solution.py:172
  483.5 21.2 %multiply_convert_fusion.3 = bf16[12,512,1024]{2,1,0:T(8,128)(2,1)} fusion(f32[12,512,1024]{2,1,0:T(8,128)} %get-tuple-element.600, f32[12,512,1024]{2,1,0:T(8,128)} %fusion.131, f32[12,512]{1,0:T(8,128)S(1)} %get-tuple-element.601, f32[12,512]{1,0:T(8,128)S(1)} %dynamic-slice_bitcast_fusion.2, pred[512,1024]{1,0:T(8,128)(4,1)S(1)} %fusion.132), kind=kLoop, calls=%fused_computation.20.clone.1 | loop fusion | flops 37748736 | bytes 63488000 | tf_op jit(solution)/shard_map/while/body/eval_jaxpr/convert_element_type | solution.py:176
  517.4 28.8 %dynamic_update_slice.59 = f32[2,512,12,64]{1,0,3,2:T(2,128)} dynamic-update-slice(f32[2,512,12,64]{1,0,3,2:T(2,128)} %get-tuple-element.657, f32[1,512,12,64]{1,0,3,2:T(1,128)S(1)} %copy.127, s32[]{:T(128)} %get-tuple-element.654, s32[]{:T(128)} %constant.86.clone.1..sunk, s32[]{:T(128)} %constant.86.clone.1..sunk, s32[]{:T(128)} %constant.86.clone.1..sunk) | dynamic-update-slice | bytes 3145732 | tf_op jit(solution)/shard_map/while/body/jit(dynamic_update_index_in_dim)/dynamic_update_slice | solution.py:141
  556.0 14.3 %bitcast_add_fusion.5 = f32[1024,12,64]{0,2,1:T(8,128)} fusion(f32[1024,12,64]{0,2,1:T(8,128)} %get-tuple-element.656, f32[12,512,1024]{2,1,0:T(8,128)} %fusion.131, f32[12,512]{1,0:T(8,128)S(1)} %dynamic-slice_bitcast_fusion.2, pred[512,1024]{1,0:T(8,128)(4,1)S(1)} %copy-done.5, pred[]{:T(512)S(6)} %compare.10, ...), kind=kOutput, calls=%fused_computation.26.clone.1 | convolution fusion | flops 832045056 | bytes 32800772 | tf_op jit(solution)/shard_map/while/body/eval_jaxpr/hqk,qhd->khd/dot_general | solution.py:188
  588.0 10.6 fusion.67
  613.4 26.4 %collective-permute-done = bf16[384,768]{1,0:T(8,128)(2,1)S(1)} collective-permute-done((bf16[384,768]{1,0:T(8,128)(2,1)}, bf16[384,768]{1,0:T(8,128)(2,1)S(1)}, u32[]{:S(2)}, u32[]{:S(2)}) %collective-permute-start) | collective-permute-done | bytes 589856 | tf_op jit(solution)/shard_map/ppermute | solution.py:23
  645.3 25.7 %collective-permute-done.2 = bf16[384,768]{1,0:T(8,128)(2,1)} collective-permute-done((bf16[384,768]{1,0:T(8,128)(2,1)S(1)}, bf16[384,768]{1,0:T(8,128)(2,1)}, u32[]{:S(2)}, u32[]{:S(2)}) %collective-permute-start.2) | collective-permute-done | bytes 589856 | tf_op jit(solution)/shard_map/ppermute | solution.py:23
  676.5 23.0 %collective-permute-start.5 = (bf16[384,768]{1,0:T(8,128)(2,1)}, bf16[384,768]{1,0:T(8,128)(2,1)S(1)}, u32[]{:S(2)}, u32[]{:S(2)}) collective-permute-start(bf16[384,768]{1,0:T(8,128)(2,1)} %collective-permute-done.3), channel_id=1, source_target_pairs={{0,28},{4,0},{8,4},{12,8},{16,12},{20,16},{24,20},{28,24},{1,29},{... | collective-permute-start | bytes 1769480 | tf_op jit(solution)/shard_map/ppermute | solution.py:28
  700.3 11.5 collective-permute-done.4
  746.4 9.9 fusion.58
  758.0 21.7 %reduce-scatter.5.cloned.1.call-done = f32[96,2304]{1,0:T(8,128)} async-done(((f32[768,2304]{1,0:T(8,128)}), f32[96,2304]{1,0:T(8,128)}) %reduce-scatter.5.cloned.1.call-update) | async-done | bytes 884752 | tf_op jit(solution)/shard_map/reduce_scatter | solution.py:341
  781.6 164.6 %reduce-scatter.9.cloned.1.call-done = f32[96,3072]{1,0:T(8,128)} async-done(((f32[768,3072]{1,0:T(8,128)}), f32[96,3072]{1,0:T(8,128)}) %reduce-scatter.9.cloned.1.call-update) | async-done | bytes 1179664 | tf_op jit(solution)/shard_map/reduce_scatter | solution.py:306
  948.4 164.4 %reduce-scatter.11.cloned.1.call-done = f32[384,768]{1,0:T(8,128)} async-done(((f32[3072,768]{1,0:T(8,128)}), f32[384,768]{1,0:T(8,128)}) %reduce-scatter.11.cloned.1.call-update) | async-done | bytes 1179664 | tf_op jit(solution)/shard_map/reduce_scatter | solution.py:308
  1123.5 35.8 %all-reduce.15 = (bf16[768]{0:T(1024)(128)(2,1)S(1)}, bf16[768]{0:T(1024)(128)(2,1)S(1)}, bf16[2304]{0:T(1024)(128)(2,1)S(1)}, bf16[768]{0:T(1024)(128)(2,1)S(1)...) all-reduce(f32[768]{0:T(1024)S(1)} %get-tuple-element.321, ...), channel_id=2, replica_groups=mesh['fsdp'=8,'replica'=4] {'fsdp'}, use_global_device_ids=true, to_apply=%region_19.20.clone | all-reduce | flops 9984 | bytes 59904
  (358 shorter events, 267.4 us)
Async XLA Ops:
  7.2 87.4 %all-gather.6.cloned.1.call-start = ((), (), s32[]{:S(2)}) async-start(), calls=%async_computation.4 | async-start | bytes 3981312 | tf_op jit(solution)/shard_map/all_gather | solution.py:230
  7.9 192.2 %all-gather.8.cloned.1.call-start = ((), (), s32[]{:S(2)}) async-start(), calls=%async_computation.5 | async-start | bytes 1327104 | tf_op jit(solution)/shard_map/all_gather | solution.py:232
  8.7 195.8 %all-gather.10.cloned.1.call-start = ((), (), s32[]{:S(2)}) async-start(), calls=%async_computation.6 | async-start | bytes 5308416 | tf_op jit(solution)/shard_map/all_gather | solution.py:238
  9.4 272.2 %all-gather.12.cloned.1.call-start = ((), (), s32[]{:S(2)}) async-start(), calls=%async_computation.7 | async-start | bytes 5308416 | tf_op jit(solution)/shard_map/all_gather | solution.py:290
  10.0 746.4 %reduce-scatter.7.cloned.1.call-start = ((), (), s32[]{:S(2)}) async-start(), calls=%async_computation.9 | async-start | bytes 2654208 | tf_op jit(solution)/shard_map/reduce_scatter | solution.py:343
  58.2 36.3 %copy-start.48 = (f32[768]{0:T(1024)}, f32[768]{0:T(1024)S(1)}, u32[]{:S(2)}) copy-start(f32[768]{0:T(1024)S(1)} %convert_element_type.174) | copy-start | bytes 9220
  58.2 36.3 %copy-start.67 = (f32[768]{0:T(1024)}, f32[768]{0:T(1024)S(1)}, u32[]{:S(2)}) copy-start(f32[768]{0:T(1024)S(1)} %convert_element_type.175) | copy-start | bytes 9220
  58.3 33.4 %copy-start.26 = (bf16[1,1024,768]{2,1,0:T(8,128)(2,1)S(1)}, bf16[1,1024,768]{2,1,0:T(8,128)(2,1)}, u32[]{:S(2)}) copy-start(bf16[1,1024,768]{2,1,0:T(8,128)(2,1)} %param.21) | copy-start | bytes 4718596
  60.1 34.4 %copy-start.8 = (bf16[1,1024,768]{1,2,0:T(8,128)(2,1)}, bf16[1,1024,768]{1,2,0:T(8,128)(2,1)S(1)}, u32[]{:S(2)}) copy-start(bf16[1,1024,768]{1,2,0:T(8,128)(2,1)S(1)} %copy.84) | copy-start | bytes 4718596
  60.4 40.5 %copy-start.46 = (f32[1024]{0:T(1024)}, f32[1024]{0:T(1024)S(1)}, u32[]{:S(2)}) copy-start(f32[1024]{0:T(1024)S(1)} %broadcast_multiply_fusion.1) | copy-start | bytes 12292
  60.9 40.0 %copy-start.52 = (f32[1024]{0:T(1024)}, f32[1024]{0:T(1024)S(1)}, u32[]{:S(2)}) copy-start(f32[1024]{0:T(1024)S(1)} %fusion.61) | copy-start | bytes 12292
  122.4 23.5 %copy-start.7 = (bf16[1024,12,64]{0,2,1:T(8,128)(2,1)S(1)}, bf16[1024,12,64]{0,2,1:T(8,128)(2,1)}, u32[]{:S(2)}) copy-start(bf16[1024,12,64]{0,2,1:T(8,128)(2,1)} %get-tuple-element.636) | copy-start | bytes 4718596 | tf_op jit(solution)/shard_map/while
  204.0 113.9 %copy-start.13 = (f32[1024,768]{0,1:T(8,128)}, f32[1024,768]{0,1:T(8,128)S(1)}, u32[]{:S(2)}) copy-start(f32[1024,768]{0,1:T(8,128)S(1)} %get-tuple-element.432) | copy-start | bytes 9437188
  204.0 113.9 %copy-start.50 = (f32[1024]{0:T(1024)}, f32[1024]{0:T(1024)S(1)}, u32[]{:S(2)}) copy-start(f32[1024]{0:T(1024)S(1)} %broadcast_multiply_fusion) | copy-start | bytes 12292
  204.4 113.5 %copy-start.60 = (f32[1024]{0:T(1024)}, f32[1024]{0:T(1024)S(1)}, u32[]{:S(2)}) copy-start(f32[1024]{0:T(1024)S(1)} %fusion.62) | copy-start | bytes 12292
  324.4 455.3 %reduce-scatter.5.cloned.1.call-start = ((), (), s32[]{:S(2)}) async-start(), calls=%async_computation.8 | async-start | bytes 7962624 | tf_op jit(solution)/shard_map/reduce_scatter | solution.py:341
  335.8 30.1 %copy-start.4 = (pred[512,1024]{1,0:T(8,128)(4,1)}, pred[512,1024]{1,0:T(8,128)(4,1)S(1)}, u32[]{:S(2)}) copy-start(pred[512,1024]{1,0:T(8,128)(4,1)S(1)} %fusion.132) | copy-start | bytes 1572868 | tf_op jit(solution)/shard_map/while
  453.9 29.6 %copy-start.4 = (pred[512,1024]{1,0:T(8,128)(4,1)}, pred[512,1024]{1,0:T(8,128)(4,1)S(1)}, u32[]{:S(2)}) copy-start(pred[512,1024]{1,0:T(8,128)(4,1)S(1)} %fusion.132) | copy-start | bytes 1572868 | tf_op jit(solution)/shard_map/while
  579.0 153.6 %copy-start.21 = (bf16[1024,12,64]{0,2,1:T(8,128)(2,1)}, bf16[1024,12,64]{0,2,1:T(8,128)(2,1)S(1)}, u32[]{:S(2)}) copy-start(bf16[1024,12,64]{0,2,1:T(8,128)(2,1)S(1)} %get-tuple-element.440) | copy-start | bytes 4718596
  587.3 358.9 %reduce-scatter.9.cloned.1.call-start = ((), (), s32[]{:S(2)}) async-start(), calls=%async_computation.10 | async-start | bytes 10616832 | tf_op jit(solution)/shard_map/reduce_scatter | solution.py:306
  598.6 514.2 %reduce-scatter.11.cloned.1.call-start = ((), (), s32[]{:S(2)}) async-start(), calls=%async_computation.11 | async-start | bytes 10616832 | tf_op jit(solution)/shard_map/reduce_scatter | solution.py:308
  608.5 64.4 %copy-start.72 = (bf16[768]{0:T(1024)(128)(2,1)S(1)}, bf16[768]{0:T(1024)(128)(2,1)}, u32[]{:S(2)}) copy-start(bf16[768]{0:T(1024)(128)(2,1)} %get-tuple-element.381) | copy-start | bytes 4612
  608.6 565.4 %all-reduce.21.cloned.1.call-start = ((), (), s32[]{:S(2)}) async-start(), calls=%async_computation.12 | async-start | bytes 3538944 | tf_op jit(solution)/shard_map/psum | solution.py:349
  608.6 31.1 %collective-permute-start = (bf16[384,768]{1,0:T(8,128)(2,1)}, bf16[384,768]{1,0:T(8,128)(2,1)S(1)}, u32[]{:S(2)}, u32[]{:S(2)}) collective-permute-start(bf16[384,768]{1,0:T(8,128)(2,1)} %param.34), channel_id=1, source_target_pairs={{0,4},{4,8},{8,12},{12,16},{16,20},{20,24},{24,28},{28,0},{1,5},{5... | collective-permute-start | bytes 1769480 | tf_op jit(solution)/shard_map/ppermute | solution.py:23
  609.2 32.9 %collective-permute-start.1 = (bf16[384,768]{1,0:T(8,128)(2,1)}, bf16[384,768]{1,0:T(8,128)(2,1)}, u32[]{:S(2)}, u32[]{:S(2)}) collective-permute-start(bf16[384,768]{1,0:T(8,128)(2,1)} %param.34), channel_id=1, source_target_pairs={{0,28},{4,0},{8,4},{12,8},{16,12},{20,16},{24,20},{28,24},{1,29},{... | collective-permute-start | bytes 1769480 | tf_op jit(solution)/shard_map/ppermute | solution.py:28
  640.6 30.5 %collective-permute-start.2 = (bf16[384,768]{1,0:T(8,128)(2,1)S(1)}, bf16[384,768]{1,0:T(8,128)(2,1)}, u32[]{:S(2)}, u32[]{:S(2)}) collective-permute-start(bf16[384,768]{1,0:T(8,128)(2,1)S(1)} %collective-permute-done), channel_id=1, source_target_pairs={{0,4},{4,8},{8,12},{12,16},{16,20},{20,24},{24,28},{28,0},{1,5},{5... | collective-permute-start | bytes 1769480 | tf_op jit(solution)/shard_map/ppermute | solution.py:23
  642.1 34.4 %collective-permute-start.3 = (bf16[384,768]{1,0:T(8,128)(2,1)}, bf16[384,768]{1,0:T(8,128)(2,1)}, u32[]{:S(2)}, u32[]{:S(2)}) collective-permute-start(bf16[384,768]{1,0:T(8,128)(2,1)} %collective-permute-done.1), channel_id=1, source_target_pairs={{0,28},{4,0},{8,4},{12,8},{16,12},{20,16},{24,20},{28,24},{1,29},{... | collective-permute-start | bytes 1769480 | tf_op jit(solution)/shard_map/ppermute | solution.py:28
  671.0 40.7 %collective-permute-start.4 = (bf16[384,768]{1,0:T(8,128)(2,1)}, bf16[384,768]{1,0:T(8,128)(2,1)}, u32[]{:S(2)}, u32[]{:S(2)}) collective-permute-start(bf16[384,768]{1,0:T(8,128)(2,1)} %collective-permute-done.2), channel_id=1, source_target_pairs={{0,4},{4,8},{8,12},{12,16},{16,20},{20,24},{24,28},{28,0},{1,5},{5... | collective-permute-start | bytes 1769480 | tf_op jit(solution)/shard_map/ppermute | solution.py:23
  673.0 26.4 %copy-start.34 = (bf16[384,768]{1,0:T(8,128)(2,1)S(1)}, bf16[384,768]{1,0:T(8,128)(2,1)}, u32[]{:S(2)}) copy-start(bf16[384,768]{1,0:T(8,128)(2,1)} %copy-done.33) | copy-start | bytes 1769476
  676.5 46.0 %collective-permute-start.5 = (bf16[384,768]{1,0:T(8,128)(2,1)}, bf16[384,768]{1,0:T(8,128)(2,1)S(1)}, u32[]{:S(2)}, u32[]{:S(2)}) collective-permute-start(bf16[384,768]{1,0:T(8,128)(2,1)} %collective-permute-done.3), channel_id=1, source_target_pairs={{0,28},{4,0},{8,4},{12,8},{16,12},{20,16},{24,20},{28,24},{1,29},{... | collective-permute-start | bytes 1769480 | tf_op jit(solution)/shard_map/ppermute | solution.py:28
  711.8 20.0 %collective-permute-start.6 = (bf16[384,768]{1,0:T(8,128)(2,1)}, bf16[384,768]{1,0:T(8,128)(2,1)S(1)}, u32[]{:S(2)}, u32[]{:S(2)}) collective-permute-start(bf16[384,768]{1,0:T(8,128)(2,1)} %collective-permute-done.4), channel_id=1, source_target_pairs={{0,4},{4,8},{8,12},{12,16},{16,20},{20,24},{24,28},{28,0},{1,5},{5... | collective-permute-start | bytes 1769480 | tf_op jit(solution)/shard_map/ppermute | solution.py:23
  1123.4 49.0 %copy-start.27 = (bf16[1,1024,768]{1,2,0:T(8,128)(2,1)S(1)}, bf16[1,1024,768]{1,2,0:T(8,128)(2,1)}, u32[]{:S(2)}) copy-start(bf16[1,1024,768]{1,2,0:T(8,128)(2,1)} %fusion.58) | copy-start | bytes 4718596
  (66 other events, 337.2 us)
Sparse Core Ops, SparseCore 0:
  10.2 68.5 all-gather.5
  81.0 39.6 all-gather.7
  122.8 78.6 all-gather.9
  203.6 78.0 all-gather.11
  324.5 67.1 reduce-scatter.6
  587.4 192.1 reduce-scatter.4
  783.7 162.4 reduce-scatter.8
  950.2 162.5 reduce-scatter.10
  1116.7 45.7 all-reduce.20
